TPU v7x, 32 devices: a whole 2x2x4 slice. The times are simulated.
32 devices in a mesh: blk: 8 (over y, x, core), grp: 4 (over z).
Axes of the slice: x: 2, y: 2, z: 4, core: 2. Of those that a mesh axis runs over, the one named last changes fastest.
Arguments:
- currents: bfloat16 [4, 16, 65536], P('grp', None, 'blk'), may hold values from -6 to 6
- background: float32 [4, 16, 65536], P('grp', None, 'blk'), may hold values from -6 to 6
- green: bfloat16 [4, 512, 8, 128, 128], P('grp', 'blk'), may hold values from -0.1875 to 0.1875
- offsets: int32 [4, 512, 8], P('grp', 'blk'), may hold values from -128 to 128
- station_cells: int32 [2048, 4], P(('blk', 'grp')), may hold values from 0 to 2047, as said below
- station_green: bfloat16 [2048, 4, 128], P(('blk', 'grp')), may hold values from -0.25 to 0.25
- station_background: float32 [16, 2048], P(None, ('blk', 'grp')), may hold values from -6 to 6
Outputs:
- cell_field: float32 [4, 16, 65536], P('grp', None, 'blk')
- station_field: float32 [16, 2048], P(None, ('blk', 'grp'))
Inputs may be any that keep to these rules, and one draw needn't show every extreme that they name: `station_cells`: station s lies with device flat index s // 64; its near blocks lie in blocks from (s // 256 - 1) * 64 to (s // 256 + 2) * 64 - 1, taken modulo 512, in any slab.
All inputs are finite; a program needn't handle non-finite values.
Results may differ from a plain program's by a relative error of at most 0.0003.
Values may be sent and summed in bfloat16 or wider, within the bound.
A program may use at most 64 MiB of HBM per device.

v0:
```python
import jax
import jax.numpy as jnp
from jax import lax
from jax.sharding import PartitionSpec as P

REACH = 2


def from_behind(array, axis, by):
    peers = lax.axis_size(axis)
    return lax.ppermute(array, axis, [(i, (i + by) % peers) for i in range(peers)])


def body(currents, background, green, offsets, station_cells, station_green, station_background):
    local = currents[0]
    n_cols = local.shape[0]
    blocks = green.shape[1]
    cells = green.shape[3]
    span = blocks * cells
    here = lax.axis_index("blk")
    slab_blocks = blocks * lax.axis_size("blk")
    upper = []
    lower = []
    moving = local
    for step in range(REACH):
        moving = from_behind(moving, "blk", -1)
        upper.append(moving)
    moving = local
    for step in range(REACH):
        moving = from_behind(moving, "blk", 1)
        lower.append(moving)
    window = jnp.concatenate(lower[::-1] + [local] + upper, axis=1)
    window_blocks = window.reshape(n_cols, (2 * REACH + 1) * blocks, cells)
    source = jnp.arange(blocks, dtype=jnp.int32)[:, None] + offsets[0] + REACH * blocks
    picked = window_blocks[:, source, :]
    anomalous = jnp.einsum("bkpq,cbkq->cbp", green[0], picked, preferred_element_type=jnp.float32)
    cell_field = background + anomalous.reshape(1, n_cols, span)
    slab_stack = lax.all_gather(currents, "grp", axis=0, tiled=True)
    below = from_behind(slab_stack, "blk", 1)
    above = from_behind(slab_stack, "blk", -1)
    near = jnp.concatenate([below, slab_stack, above], axis=2)
    n_slabs = near.shape[0]
    near_blocks = near.reshape(n_slabs, n_cols, 3 * blocks, cells)
    slab_index = station_cells // slab_blocks
    position = (station_cells % slab_blocks - (here - 1) * blocks) % slab_blocks
    chosen = near_blocks[slab_index, :, position, :]
    station_field = station_background + jnp.einsum(
        "skp,skcp->cs", station_green, chosen, preferred_element_type=jnp.float32
    )
    return (cell_field, station_field)


def solution(mesh):
    return jax.shard_map(
        body,
        mesh=mesh,
        in_specs=(
            P("grp", None, "blk"),
            P("grp", None, "blk"),
            P("grp", "blk", None, None, None),
            P("grp", "blk", None),
            P(("blk", "grp"), None),
            P(("blk", "grp"), None, None),
            P(None, ("blk", "grp")),
        ),
        out_specs=(P("grp", None, "blk"), P(None, ("blk", "grp"))),
        check_vma=False,
    )
```

profile of v0, /device:TPU:1, one launch (start us, length us, event | category | flops | bytes accessed | tf_op | source)
XLA Modules:
  0.0 79.5 jit_solution(7111683563668175119)
XLA Ops:
  7.2 0.7 all-gather.2.cloned.1.call-update
  7.9 2.7 %collective-permute-start = (bf16[16,8192]{1,0:T(8,128)(2,1)}, bf16[16,8192]{1,0:T(8,128)(2,1)S(1)}, u32[]{:S(2)}, u32[]{:S(2)}) collective-permute-start(bf16[16,8192]{1,0:T(8,128)(2,1)} %bitcast.59), channel_id=1, source_target_pairs={{0,4},{4,8},{8,12},{12,16},{16,20},{20,24},{24,28},{28,0},{1,5},{5... | collective-permute-start | bytes 786440 | tf_op jit(solution)/shard_map/ppermute | solution.py:11
  10.6 1.0 %copy.39 = bf16[2,8,64,128]{3,2,1,0:T(8,128)(2,1)S(1)} copy(bf16[2,8,64,128]{3,1,2,0:T(8,128)(2,1)} %bitcast.61) | data formatting | bytes 524288
  11.6 0.7 compare_select_fusion
  12.3 0.1 copy.27
  12.4 0.1 reshape.50
  12.5 3.5 %collective-permute-done = bf16[16,8192]{1,0:T(8,128)(2,1)S(1)} collective-permute-done((bf16[16,8192]{1,0:T(8,128)(2,1)}, bf16[16,8192]{1,0:T(8,128)(2,1)S(1)}, u32[]{:S(2)}, u32[]{:S(2)}) %collective-permute-start) | collective-permute-done | bytes 262176 | tf_op jit(solution)/shard_map/ppermute | solution.py:11
  16.0 2.4 %collective-permute-start.1 = (bf16[16,8192]{1,0:T(8,128)(2,1)S(1)}, bf16[16,8192]{1,0:T(8,128)(2,1)S(1)}, u32[]{:S(2)}, u32[]{:S(2)}) collective-permute-start(bf16[16,8192]{1,0:T(8,128)(2,1)S(1)} %collective-permute-done), channel_id=1, source_target_pairs={{0,4},{4,8},{8,12},{12,16},{16,20},{20,24},{24,28},{28,0},{1,5},{5... | collective-permute-start | bytes 786440 | tf_op jit(solution)/shard_map/ppermute | solution.py:11
  18.3 0.7 fusion.11
  19.1 0.1 copy.29
  19.2 0.1 reshape.56
  19.3 0.1 collective-permute-start.3
  19.3 3.1 %collective-permute-done.1 = bf16[16,8192]{1,0:T(8,128)(2,1)S(1)} collective-permute-done((bf16[16,8192]{1,0:T(8,128)(2,1)S(1)}, bf16[16,8192]{1,0:T(8,128)(2,1)S(1)}, u32[]{:S(2)}, u32[]{:S(2)}) %collective-permute-start.1) | collective-permute-done | bytes 262176 | tf_op jit(solution)/shard_map/ppermute | solution.py:11
  22.5 0.1 bitcast_dynamic-update-slice_fusion.2
  22.6 0.2 copy_dynamic-update-slice_fusion
  22.8 0.1 bitcast_dynamic-update-slice_fusion.1
  22.9 16.6 %all-gather.2.cloned.1.call-done = bf16[4,16,8192]{2,1,0:T(8,128)(2,1)} async-done(((bf16[1,16,8192]{2,1,0:T(8,128)(2,1)}), bf16[4,16,8192]{2,1,0:T(8,128)(2,1)}) %all-gather.2.cloned.1.call-update) | async-done | bytes 1048592 | tf_op jit(solution)/shard_map/all_gather | solution.py:38
  39.5 1.9 %collective-permute-start.4 = (bf16[4,16,8192]{2,1,0:T(8,128)(2,1)}, bf16[4,16,8192]{2,1,0:T(8,128)(2,1)}, u32[]{:S(2)}, u32[]{:S(2)}) collective-permute-start(bf16[4,16,8192]{2,1,0:T(8,128)(2,1)} %all-gather.2.cloned.1.call-done), channel_id=1, source_target_pairs={{0,4},{4,8},{8,12},{12,16},{16,20},{20,24},{24,28},{28,0},{1,5},{5... | collective-permute-start | bytes 3145736 | tf_op jit(solution)/shard_map/ppermute | solution.py:11
  41.4 0.1 bitcast_dynamic-update-slice_fusion
  41.5 2.0 %gather_fusion = bf16[512,16,128]{2,1,0:T(8,128)(2,1)S(1)} fusion(bf16[16,320,128]{2,0,1:T(8,128)(2,1)S(1)} %bitcast_dynamic-update-slice_fusion, s32[1024]{0:T(1024)S(1)} %pad_clamp_fusion), kind=kCustom, calls=%fused_computation | custom fusion | bytes 4196352 | tf_op jit(solution)/shard_map/gather | solution.py:35
  43.5 8.1 %fusion.2 = f32[16,64,128]{2,0,1:T(8,128)S(1)} fusion(bf16[16,64,8,128]{3,0,2,1:T(8,128)(2,1)S(1)} %bitcast.57, bf16[1,64,8,128,128]{4,3,2,1,0:T(8,128)(2,1)} %param.9), kind=kOutput, calls=%fused_computation.6 | convolution fusion | flops 268435456 | bytes 19398656 | tf_op jit(solution)/shard_map/bkpq,cbkq->cbp/dot_general | solution.py:36
  51.6 0.2 copy.28
  51.8 0.1 reshape.46
  51.9 0.8 copy-done.2
  52.6 0.8 %add.79 = f32[1,16,8192]{2,1,0:T(8,128)} add(f32[1,16,8192]{2,1,0:T(8,128)S(1)} %copy-done.2, f32[1,16,8192]{2,1,0:T(8,128)S(1)} %reshape.46) | non-fusion elementwise | flops 131072 | bytes 1572864 | tf_op jit(solution)/shard_map/add | solution.py:37
  53.5 9.4 %collective-permute-done.4 = bf16[4,16,8192]{2,1,0:T(8,128)(2,1)} collective-permute-done((bf16[4,16,8192]{2,1,0:T(8,128)(2,1)}, bf16[4,16,8192]{2,1,0:T(8,128)(2,1)}, u32[]{:S(2)}, u32[]{:S(2)}) %collective-permute-start.4) | collective-permute-done | bytes 1048608 | tf_op jit(solution)/shard_map/ppermute | solution.py:11
  62.9 3.4 %collective-permute-done.5 = bf16[4,16,8192]{2,1,0:T(8,128)(2,1)} collective-permute-done((bf16[4,16,8192]{2,1,0:T(8,128)(2,1)}, bf16[4,16,8192]{2,1,0:T(8,128)(2,1)}, u32[]{:S(2)}, u32[]{:S(2)}) %collective-permute-start.5) | collective-permute-done | bytes 1048608 | tf_op jit(solution)/shard_map/ppermute | solution.py:11
  66.3 1.8 %copy_bitcast_fusion = bf16[4,16,192,128]{3,1,2,0:T(8,128)(2,1)S(1)} fusion(bf16[4,16,8192]{2,1,0:T(8,128)(2,1)} %collective-permute-done.5, bf16[4,16,8192]{2,1,0:T(8,128)(2,1)S(1)} %copy-done.1, bf16[4,16,8192]{2,1,0:T(8,128)(2,1)} %collective-permute-done.4), kind=kLoop, calls=%fused_computation.4 | loop fusion | flops 9437184 | bytes 6291456 | tf_op jit(solution)/shard_map/reshape | solution.py:43
  68.1 2.2 %gather_fusion.1 = bf16[256,16,128]{2,1,0:T(8,128)(2,1)} fusion(bf16[4,16,192,128]{3,1,2,0:T(8,128)(2,1)S(1)} %copy_bitcast_fusion, s32[256]{0:T(256)S(1)} %reshape.56), kind=kCustom, calls=%fused_computation.1 | custom fusion | bytes 2099200 | tf_op jit(solution)/shard_map/gather | solution.py:46
  70.3 1.6 %fusion.5 = f32[64,1,16,1]{2,1,3,0:T(1,128)S(1)} fusion(bf16[64,4,16,128]{3,2,1,0:T(8,128)(2,1)} %bitcast.58, bf16[64,4,128,1]{2,1,0,3:T(4,128)(2,1)S(1)} %bitcast.56), kind=kOutput, calls=%fused_computation.12 | convolution fusion | flops 1048576 | bytes 1118208 | tf_op jit(solution)/shard_map/skp,skcp->cs/dot_general | solution.py:47
  72.0 0.1 copy.33
  72.0 0.6 bitcast_add_fusion
  (14 shorter events, 0.1 us)
Async XLA Ops:
  7.2 63.2 %copy-start = (bf16[64,4,128]{2,1,0:T(4,128)(2,1)S(1)}, bf16[64,4,128]{2,1,0:T(4,128)(2,1)}, u32[]{:S(2)}) copy-start(bf16[64,4,128]{2,1,0:T(4,128)(2,1)} %param.12) | copy-start | bytes 196612
  7.2 32.3 %all-gather.2.cloned.1.call-start = ((), (), s32[]{:S(2)}) async-start(), calls=%async_computation | async-start | bytes 1310720 | tf_op jit(solution)/shard_map/all_gather | solution.py:38
  7.9 8.1 %collective-permute-start = (bf16[16,8192]{1,0:T(8,128)(2,1)}, bf16[16,8192]{1,0:T(8,128)(2,1)S(1)}, u32[]{:S(2)}, u32[]{:S(2)}) collective-permute-start(bf16[16,8192]{1,0:T(8,128)(2,1)} %bitcast.59), channel_id=1, source_target_pairs={{0,4},{4,8},{8,12},{12,16},{16,20},{20,24},{24,28},{28,0},{1,5},{5... | collective-permute-start | bytes 786440 | tf_op jit(solution)/shard_map/ppermute | solution.py:11
  10.6 8.7 %collective-permute-start.2 = (bf16[16,8192]{1,0:T(8,128)(2,1)}, bf16[16,8192]{1,0:T(8,128)(2,1)S(1)}, u32[]{:S(2)}, u32[]{:S(2)}) collective-permute-start(bf16[16,8192]{1,0:T(8,128)(2,1)} %bitcast.60), channel_id=1, source_target_pairs={{0,28},{4,0},{8,4},{12,8},{16,12},{20,16},{24,20},{28,24},{1,29},{... | collective-permute-start | bytes 786440 | tf_op jit(solution)/shard_map/ppermute | solution.py:11
  16.0 6.5 %collective-permute-start.1 = (bf16[16,8192]{1,0:T(8,128)(2,1)S(1)}, bf16[16,8192]{1,0:T(8,128)(2,1)S(1)}, u32[]{:S(2)}, u32[]{:S(2)}) collective-permute-start(bf16[16,8192]{1,0:T(8,128)(2,1)S(1)} %collective-permute-done), channel_id=1, source_target_pairs={{0,4},{4,8},{8,12},{12,16},{16,20},{20,24},{24,28},{28,0},{1,5},{5... | collective-permute-start | bytes 786440 | tf_op jit(solution)/shard_map/ppermute | solution.py:11
  19.3 22.1 %collective-permute-start.3 = (bf16[16,8192]{1,0:T(8,128)(2,1)S(1)}, bf16[16,8192]{1,0:T(8,128)(2,1)S(1)}, u32[]{:S(2)}, u32[]{:S(2)}) collective-permute-start(bf16[16,8192]{1,0:T(8,128)(2,1)S(1)} %collective-permute-done.2), channel_id=1, source_target_pairs={{0,28},{4,0},{8,4},{12,8},{16,12},{20,16},{24,20},{28,24},{1,29},{... | collective-permute-start | bytes 786440 | tf_op jit(solution)/shard_map/ppermute | solution.py:11
  39.5 23.4 %collective-permute-start.4 = (bf16[4,16,8192]{2,1,0:T(8,128)(2,1)}, bf16[4,16,8192]{2,1,0:T(8,128)(2,1)}, u32[]{:S(2)}, u32[]{:S(2)}) collective-permute-start(bf16[4,16,8192]{2,1,0:T(8,128)(2,1)} %all-gather.2.cloned.1.call-done), channel_id=1, source_target_pairs={{0,4},{4,8},{8,12},{12,16},{16,20},{20,24},{24,28},{28,0},{1,5},{5... | collective-permute-start | bytes 3145736 | tf_op jit(solution)/shard_map/ppermute | solution.py:11
  41.4 24.9 %collective-permute-start.5 = (bf16[4,16,8192]{2,1,0:T(8,128)(2,1)}, bf16[4,16,8192]{2,1,0:T(8,128)(2,1)}, u32[]{:S(2)}, u32[]{:S(2)}) collective-permute-start(bf16[4,16,8192]{2,1,0:T(8,128)(2,1)} %all-gather.2.cloned.1.call-done), channel_id=1, source_target_pairs={{0,28},{4,0},{8,4},{12,8},{16,12},{20,16},{24,20},{28,24},{1,29},{... | collective-permute-start | bytes 3145736 | tf_op jit(solution)/shard_map/ppermute | solution.py:11
  51.6 1.1 %copy-start.2 = (f32[1,16,8192]{2,1,0:T(8,128)S(1)}, f32[1,16,8192]{2,1,0:T(8,128)}, u32[]{:S(2)}) copy-start(f32[1,16,8192]{2,1,0:T(8,128)} %param.8) | copy-start | bytes 1572868
  52.6 13.7 %copy-start.1 = (bf16[4,16,8192]{2,1,0:T(8,128)(2,1)S(1)}, bf16[4,16,8192]{2,1,0:T(8,128)(2,1)}, u32[]{:S(2)}) copy-start(bf16[4,16,8192]{2,1,0:T(8,128)(2,1)} %all-gather.2.cloned.1.call-done) | copy-start | bytes 3145732
  68.1 3.9 %copy-start.3 = (f32[16,64]{1,0:T(8,128)S(1)}, f32[16,64]{1,0:T(8,128)}, u32[]{:S(2)}) copy-start(f32[16,64]{1,0:T(8,128)} %param.13) | copy-start | bytes 12292
Sparse Core Ops, SparseCore 0:
  9.6 29.8 all-gather.1
where the time goes:
time: 79.8 us; the launch traced here: 79.5 us
  waiting for transfers between devices  36.8 us (46%)
  between operations  14.2 us (18%)
  matrix products  9.71 us (12%)
  local copies, waits for them, and re-layouts  7.17 us (9%)
  starting transfers between devices  7.01 us (9%)
  other arithmetic  4.68 us (6%)
    ppermute x6, waiting for transfers between devices, from_behind(): lax.ppermute(array, axis, [(i, (i + by) % peers) for i in range(peers)])  19.5 us
    all_gather x1, waiting for transfers between devices, body(): slab_stack = lax.all_gather(currents, 'grp', axis=0, tiled=True)  16.6 us
    dot_general x1, matrix products, body(): jnp.einsum('bkpq,cbkq->cbp', green[0], picked, preferred_element_type=jnp...  8.07 us
    ppermute x6, starting transfers between devices, from_behind(): lax.ppermute(array, axis, [(i, (i + by) % peers) for i in range(peers)])  6.98 us
    gather x1, local copies, waits for them, and re-layouts, body(): chosen = near_blocks[slab_index, :, position, :]  2.19 us
    unnamed x13, local copies, waits for them, and re-layouts  2.17 us
    gather x1, local copies, waits for them, and re-layouts, body(): picked = window_blocks[:, source, :]  2.02 us
    reshape x1, other arithmetic, body(): near_blocks = near.reshape(n_slabs, n_cols, 3 * blocks, cells)  1.81 us
  transfers between devices with their start and end apart: 7, of which 5 were waited for; matrix products, arithmetic and copies ran while one was open for 18% of the time, Pallas kernels for 0%

commit v1 on v0

--- a/solution.py
+++ b/solution.py
@@ -4,6 +4,24 @@
 from jax.sharding import PartitionSpec as P
 
 REACH = 2
+
+
+def in_order(tiles, dim):
+    dims = list(tiles.shape[1:])
+    dims[dim] *= tiles.shape[0]
+    return jnp.moveaxis(tiles, 0, dim).reshape(dims)
+
+
+def grow_blocks(shard, axis):
+    size = lax.axis_size(axis)
+    parts = shard[None]
+    for level in range(size.bit_length() - 1):
+        stride = 1 << level
+        partner_block = lax.ppermute(parts, axis, [(i, i ^ stride) for i in range(size)])
+        both = jnp.stack([parts, partner_block])
+        upper = lax.axis_index(axis) >> level & 1
+        parts = jnp.where(upper == 0, both, both[::-1]).reshape(-1, *shard.shape)
+    return parts
 
 
 def from_behind(array, axis, by):
@@ -35,7 +53,7 @@
     picked = window_blocks[:, source, :]
     anomalous = jnp.einsum("bkpq,cbkq->cbp", green[0], picked, preferred_element_type=jnp.float32)
     cell_field = background + anomalous.reshape(1, n_cols, span)
-    slab_stack = lax.all_gather(currents, "grp", axis=0, tiled=True)
+    slab_stack = in_order(grow_blocks(currents, "grp"), 0)
     below = from_behind(slab_stack, "blk", 1)
     above = from_behind(slab_stack, "blk", -1)
     near = jnp.concatenate([below, slab_stack, above], axis=2)

time: 79.8 us -> 74.6 us (0.935)
  the two profiles are of different devices: /device:TPU:1 before, /device:TPU:0 now
where the time goes in v1:
time: 74.6 us; the launch traced here: 74.2 us
  waiting for transfers between devices  33.8 us (45%)
  starting transfers between devices  12.2 us (16%)
  local copies, waits for them, and re-layouts  12.1 us (16%)
  matrix products  9.7 us (13%)
  other arithmetic  5.6 us (8%)
  between operations  0.79 us (1%)
    ppermute x2, waiting for transfers between devices, grow_blocks(): lax.ppermute(parts, axis, [(i, i ^ stride) for i in range(size)])  22.5 us
    ppermute x6, waiting for transfers between devices, from_behind(): lax.ppermute(array, axis, [(i, (i + by) % peers) for i in range(peers)])  11.3 us
    dot_general x1, matrix products, body(): jnp.einsum('bkpq,cbkq->cbp', green[0], picked, preferred_element_type=jnp...  8.06 us
    ppermute x6, starting transfers between devices, from_behind(): lax.ppermute(array, axis, [(i, (i + by) % peers) for i in range(peers)])  7.31 us
    ppermute x2, starting transfers between devices, grow_blocks(): lax.ppermute(parts, axis, [(i, i ^ stride) for i in range(size)])  4.92 us
    unnamed x12, local copies, waits for them, and re-layouts  3.63 us
    concatenate x3, local copies, waits for them, and re-layouts, body(): near = jnp.concatenate([below, slab_stack, above], axis=2)  3.49 us
    gather x1, local copies, waits for them, and re-layouts, body(): chosen = near_blocks[slab_index, :, position, :]  2.18 us
  transfers between devices with their start and end apart: 8, of which 5 were waited for; matrix products, arithmetic and copies ran while one was open for 27% of the time, Pallas kernels for 0%

profile of v1, /device:TPU:0, one launch (start us, length us, event | category | flops | bytes accessed | tf_op | source)
XLA Modules:
  0.0 74.2 jit_solution(2370050028861201693)
XLA Ops:
  0.6 0.5 collective-permute-start
  1.1 2.9 %collective-permute-start.2 = (bf16[16,8192]{1,0:T(8,128)(2,1)}, bf16[16,8192]{1,0:T(8,128)(2,1)S(1)}, u32[]{:S(2)}, u32[]{:S(2)}) collective-permute-start(bf16[16,8192]{1,0:T(8,128)(2,1)} %bitcast.82), channel_id=1, source_target_pairs={{0,28},{4,0},{8,4},{12,8},{16,12},{20,16},{24,20},{28,24},{1,29},{... | collective-permute-start | bytes 786440 | tf_op jit(solution)/shard_map/ppermute | solution.py:29
  4.1 2.3 %collective-permute-start.4 = (bf16[1,1,16,8192]{3,2,1,0:T(8,128)(2,1)}, bf16[1,1,16,8192]{3,2,1,0:T(8,128)(2,1)S(1)}, u32[]{:S(2)}, u32[]{:S(2)}) collective-permute-start(bf16[1,1,16,8192]{3,2,1,0:T(8,128)(2,1)} %bitcast.83), channel_id=1, source_target_pairs={{0,1},{1,0},{2,3},{3,2},{4,5},{5,4},{6,7},{7,6},{8,9},{9,8},{10,11... | collective-permute-start | bytes 786440 | tf_op jit(solution)/shard_map/ppermute | solution.py:20
  6.4 0.7 fusion.13
  7.1 0.1 copy.23
  7.2 0.1 reshape.61
  7.3 1.0 %copy.33 = bf16[2,8,64,128]{3,2,1,0:T(8,128)(2,1)S(1)} copy(bf16[2,8,64,128]{3,1,2,0:T(8,128)(2,1)} %bitcast.84) | data formatting | bytes 524288
  8.3 0.7 compare_select_fusion
  9.2 3.0 %collective-permute-done.4 = bf16[1,1,16,8192]{3,2,1,0:T(8,128)(2,1)S(1)} collective-permute-done((bf16[1,1,16,8192]{3,2,1,0:T(8,128)(2,1)}, bf16[1,1,16,8192]{3,2,1,0:T(8,128)(2,1)S(1)}, u32[]{:S(2)}, u32[]{:S(2)}) %collective-permute-start.4) | collective-permute-done | bytes 262176 | tf_op jit(solution)/shard_map/ppermute | solution.py:20
  12.2 1.0 %pad_maximum_fusion.2 = bf16[2,1,1,16,8192]{4,3,2,1,0:T(8,128)(2,1)S(1)} fusion(bf16[1,1,1,16,8192]{4,3,2,1,0:T(8,128)(2,1)S(1)} %bitcast.87, bf16[1,1,1,16,8192]{4,3,2,1,0:T(8,128)(2,1)} %bitcast.85), kind=kLoop, calls=%fused_computation.11 | loop fusion | flops 262144 | bytes 1048576 | tf_op jit(solution)/shard_map/stack | solution.py:21
  13.4 2.7 %collective-permute-start.5 = (bf16[2,1,16,8192]{3,2,0,1:T(8,128)(2,1)S(1)}, bf16[2,1,16,8192]{3,2,0,1:T(8,128)(2,1)S(1)}, u32[]{:S(2)}, u32[]{:S(2)}) collective-permute-start(bf16[2,1,16,8192]{3,2,0,1:T(8,128)(2,1)S(1)} %get-tuple-element.3), channel_id=1, source_target_pairs={{0,2},{1,3},{2,0},{3,1},{4,6},{5,7},{6,4},{7,5},{8,10},{9,11},{10,... | collective-permute-start | bytes 1572872 | tf_op jit(solution)/shard_map/ppermute | solution.py:20
  16.0 2.3 %collective-permute-start.3 = (bf16[16,8192]{1,0:T(8,128)(2,1)S(1)}, bf16[16,8192]{1,0:T(8,128)(2,1)S(1)}, u32[]{:S(2)}, u32[]{:S(2)}) collective-permute-start(bf16[16,8192]{1,0:T(8,128)(2,1)S(1)} %collective-permute-done.2), channel_id=1, source_target_pairs={{0,28},{4,0},{8,4},{12,8},{16,12},{20,16},{24,20},{28,24},{1,29},{... | collective-permute-start | bytes 786440 | tf_op jit(solution)/shard_map/ppermute | solution.py:29
  18.4 1.6 %collective-permute-done.1 = bf16[16,8192]{1,0:T(8,128)(2,1)S(1)} collective-permute-done((bf16[16,8192]{1,0:T(8,128)(2,1)S(1)}, bf16[16,8192]{1,0:T(8,128)(2,1)S(1)}, u32[]{:S(2)}, u32[]{:S(2)}) %collective-permute-start.1) | collective-permute-done | bytes 262176 | tf_op jit(solution)/shard_map/ppermute | solution.py:29
  20.1 0.2 copy_dynamic-update-slice_fusion
  20.3 19.5 %collective-permute-done.5 = bf16[2,1,16,8192]{3,2,0,1:T(8,128)(2,1)S(1)} collective-permute-done((bf16[2,1,16,8192]{3,2,0,1:T(8,128)(2,1)S(1)}, bf16[2,1,16,8192]{3,2,0,1:T(8,128)(2,1)S(1)}, u32[]{:S(2)}, u32[]{:S(2)}) %collective-permute-start.5) | collective-permute-done | bytes 524320 | tf_op jit(solution)/shard_map/ppermute | solution.py:20
  39.9 1.1 %reverse_select_fusion = bf16[2,2,1,16,8192]{4,3,1,2,0:T(8,128)(2,1)} fusion(bf16[2,2,1,16,8192]{4,3,1,2,0:T(8,128)(2,1)S(1)} %pad_maximum_fusion.1, pred[]{:T(512)S(6)} %eq.9), kind=kLoop, calls=%fused_computation.5 | loop fusion | flops 524288 | bytes 2097153 | tf_op jit(solution)/shard_map/jit(_where)/select_n | solution.py:23
  41.0 1.4 %collective-permute-start.7 = (bf16[4,16,8192]{2,1,0:T(8,128)(2,1)}, bf16[4,16,8192]{2,1,0:T(8,128)(2,1)}, u32[]{:S(2)}, u32[]{:S(2)}) collective-permute-start(bf16[4,16,8192]{2,1,0:T(8,128)(2,1)} %bitcast.14), channel_id=1, source_target_pairs={{0,28},{4,0},{8,4},{12,8},{16,12},{20,16},{24,20},{28,24},{1,29},{... | collective-permute-start | bytes 3145736 | tf_op jit(solution)/shard_map/ppermute | solution.py:29
  42.5 2.0 %gather_fusion = bf16[512,16,128]{2,1,0:T(8,128)(2,1)S(1)} fusion(bf16[16,320,128]{2,0,1:T(8,128)(2,1)S(1)} %bitcast_dynamic-update-slice_fusion, s32[1024]{0:T(1024)S(1)} %pad_clamp_fusion), kind=kCustom, calls=%fused_computation | custom fusion | bytes 4196352 | tf_op jit(solution)/shard_map/gather | solution.py:53
  44.6 8.1 %fusion.2 = f32[16,64,128]{2,0,1:T(8,128)S(1)} fusion(bf16[16,64,8,128]{3,0,2,1:T(8,128)(2,1)S(1)} %bitcast.77, bf16[1,64,8,128,128]{4,3,2,1,0:T(8,128)(2,1)} %param.9), kind=kOutput, calls=%fused_computation.6 | convolution fusion | flops 268435456 | bytes 19398656 | tf_op jit(solution)/shard_map/bkpq,cbkq->cbp/dot_general | solution.py:54
  52.7 0.2 copy.19
  53.0 0.8 %copy-done.1 = f32[1,16,8192]{2,1,0:T(8,128)S(1)} copy-done((f32[1,16,8192]{2,1,0:T(8,128)S(1)}, f32[1,16,8192]{2,1,0:T(8,128)}, u32[]{:S(2)}) %copy-start.1) | copy-done | bytes 524312
  53.7 0.8 %add.79 = f32[1,16,8192]{2,1,0:T(8,128)} add(f32[1,16,8192]{2,1,0:T(8,128)S(1)} %copy-done.1, f32[1,16,8192]{2,1,0:T(8,128)S(1)} %reshape.51) | non-fusion elementwise | flops 131072 | bytes 1572864 | tf_op jit(solution)/shard_map/add | solution.py:55
  54.6 1.5 %copy.34 = bf16[8,8,64,128]{3,2,1,0:T(8,128)(2,1)S(1)} copy(bf16[8,8,64,128]{3,1,2,0:T(8,128)(2,1)} %bitcast.41) | data formatting | bytes 2097152
  56.1 0.7 copy.21
  56.8 7.3 %collective-permute-done.7 = bf16[4,16,8192]{2,1,0:T(8,128)(2,1)} collective-permute-done((bf16[4,16,8192]{2,1,0:T(8,128)(2,1)}, bf16[4,16,8192]{2,1,0:T(8,128)(2,1)}, u32[]{:S(2)}, u32[]{:S(2)}) %collective-permute-start.7) | collective-permute-done | bytes 1048608 | tf_op jit(solution)/shard_map/ppermute | solution.py:29
  64.1 1.4 %copy_bitcast_fusion = bf16[4,16,64,128]{3,1,2,0:T(8,128)(2,1)S(1)} fusion(bf16[4,16,8192]{2,1,0:T(8,128)(2,1)} %collective-permute-done.7), kind=kLoop, calls=%fused_computation.7 | loop fusion | bytes 2097152 | tf_op jit(solution)/shard_map/concatenate | solution.py:59
  65.5 2.4 %collective-permute-done.6 = bf16[4,16,8192]{2,1,0:T(8,128)(2,1)} collective-permute-done((bf16[4,16,8192]{2,1,0:T(8,128)(2,1)}, bf16[4,16,8192]{2,1,0:T(8,128)(2,1)}, u32[]{:S(2)}, u32[]{:S(2)}) %collective-permute-start.6) | collective-permute-done | bytes 1048608 | tf_op jit(solution)/shard_map/ppermute | solution.py:29
  67.9 1.4 %copy_bitcast_fusion.1 = bf16[4,16,64,128]{3,1,2,0:T(8,128)(2,1)S(1)} fusion(bf16[4,16,8192]{2,1,0:T(8,128)(2,1)} %collective-permute-done.6), kind=kLoop, calls=%fused_computation.8 | loop fusion | bytes 2097152 | tf_op jit(solution)/shard_map/concatenate | solution.py:59
  69.3 0.4 pad_maximum_fusion
  69.7 2.2 %gather_fusion.1 = bf16[256,16,128]{2,1,0:T(8,128)(2,1)} fusion(bf16[4,16,192,128]{3,1,2,0:T(8,128)(2,1)S(1)} %pad_maximum_fusion, s32[256]{0:T(256)S(1)} %reshape.61), kind=kCustom, calls=%fused_computation.1 | custom fusion | bytes 2099200 | tf_op jit(solution)/shard_map/gather | solution.py:64
  71.9 1.6 %fusion.7 = f32[64,1,16,1]{2,1,3,0:T(1,128)S(1)} fusion(bf16[64,4,16,128]{3,2,1,0:T(8,128)(2,1)} %bitcast.79, bf16[64,4,128,1]{2,1,0,3:T(4,128)(2,1)S(1)} %bitcast.76), kind=kOutput, calls=%fused_computation.19 | convolution fusion | flops 1048576 | bytes 1118208 | tf_op jit(solution)/shard_map/skp,skcp->cs/dot_general | solution.py:65
  73.6 0.6 bitcast_add_fusion
  (21 shorter events, 0.9 us)
Async XLA Ops:
  0.6 71.2 %copy-start = (bf16[64,4,128]{2,1,0:T(4,128)(2,1)S(1)}, bf16[64,4,128]{2,1,0:T(4,128)(2,1)}, u32[]{:S(2)}) copy-start(bf16[64,4,128]{2,1,0:T(4,128)(2,1)} %param.12) | copy-start | bytes 196612
  0.6 12.5 %collective-permute-start = (bf16[16,8192]{1,0:T(8,128)(2,1)}, bf16[16,8192]{1,0:T(8,128)(2,1)S(1)}, u32[]{:S(2)}, u32[]{:S(2)}) collective-permute-start(bf16[16,8192]{1,0:T(8,128)(2,1)} %bitcast.81), channel_id=1, source_target_pairs={{0,4},{4,8},{8,12},{12,16},{16,20},{20,24},{24,28},{28,0},{1,5},{5... | collective-permute-start | bytes 786440 | tf_op jit(solution)/shard_map/ppermute | solution.py:29
  1.1 14.9 %collective-permute-start.2 = (bf16[16,8192]{1,0:T(8,128)(2,1)}, bf16[16,8192]{1,0:T(8,128)(2,1)S(1)}, u32[]{:S(2)}, u32[]{:S(2)}) collective-permute-start(bf16[16,8192]{1,0:T(8,128)(2,1)} %bitcast.82), channel_id=1, source_target_pairs={{0,28},{4,0},{8,4},{12,8},{16,12},{20,16},{24,20},{28,24},{1,29},{... | collective-permute-start | bytes 786440 | tf_op jit(solution)/shard_map/ppermute | solution.py:29
  4.1 8.1 %collective-permute-start.4 = (bf16[1,1,16,8192]{3,2,1,0:T(8,128)(2,1)}, bf16[1,1,16,8192]{3,2,1,0:T(8,128)(2,1)S(1)}, u32[]{:S(2)}, u32[]{:S(2)}) collective-permute-start(bf16[1,1,16,8192]{3,2,1,0:T(8,128)(2,1)} %bitcast.83), channel_id=1, source_target_pairs={{0,1},{1,0},{2,3},{3,2},{4,5},{5,4},{6,7},{7,6},{8,9},{9,8},{10,11... | collective-permute-start | bytes 786440 | tf_op jit(solution)/shard_map/ppermute | solution.py:20
  13.2 6.7 %collective-permute-start.1 = (bf16[16,8192]{1,0:T(8,128)(2,1)S(1)}, bf16[16,8192]{1,0:T(8,128)(2,1)S(1)}, u32[]{:S(2)}, u32[]{:S(2)}) collective-permute-start(bf16[16,8192]{1,0:T(8,128)(2,1)S(1)} %collective-permute-done), channel_id=1, source_target_pairs={{0,4},{4,8},{8,12},{12,16},{16,20},{20,24},{24,28},{28,0},{1,5},{5... | collective-permute-start | bytes 786440 | tf_op jit(solution)/shard_map/ppermute | solution.py:29
  13.4 26.4 %collective-permute-start.5 = (bf16[2,1,16,8192]{3,2,0,1:T(8,128)(2,1)S(1)}, bf16[2,1,16,8192]{3,2,0,1:T(8,128)(2,1)S(1)}, u32[]{:S(2)}, u32[]{:S(2)}) collective-permute-start(bf16[2,1,16,8192]{3,2,0,1:T(8,128)(2,1)S(1)} %get-tuple-element.3), channel_id=1, source_target_pairs={{0,2},{1,3},{2,0},{3,1},{4,6},{5,7},{6,4},{7,5},{8,10},{9,11},{10,... | collective-permute-start | bytes 1572872 | tf_op jit(solution)/shard_map/ppermute | solution.py:20
  16.0 26.4 %collective-permute-start.3 = (bf16[16,8192]{1,0:T(8,128)(2,1)S(1)}, bf16[16,8192]{1,0:T(8,128)(2,1)S(1)}, u32[]{:S(2)}, u32[]{:S(2)}) collective-permute-start(bf16[16,8192]{1,0:T(8,128)(2,1)S(1)} %collective-permute-done.2), channel_id=1, source_target_pairs={{0,28},{4,0},{8,4},{12,8},{16,12},{20,16},{24,20},{28,24},{1,29},{... | collective-permute-start | bytes 786440 | tf_op jit(solution)/shard_map/ppermute | solution.py:29
  41.0 23.0 %collective-permute-start.7 = (bf16[4,16,8192]{2,1,0:T(8,128)(2,1)}, bf16[4,16,8192]{2,1,0:T(8,128)(2,1)}, u32[]{:S(2)}, u32[]{:S(2)}) collective-permute-start(bf16[4,16,8192]{2,1,0:T(8,128)(2,1)} %bitcast.14), channel_id=1, source_target_pairs={{0,28},{4,0},{8,4},{12,8},{16,12},{20,16},{24,20},{28,24},{1,29},{... | collective-permute-start | bytes 3145736 | tf_op jit(solution)/shard_map/ppermute | solution.py:29
  44.5 23.3 %collective-permute-start.6 = (bf16[4,16,8192]{2,1,0:T(8,128)(2,1)}, bf16[4,16,8192]{2,1,0:T(8,128)(2,1)}, u32[]{:S(2)}, u32[]{:S(2)}) collective-permute-start(bf16[4,16,8192]{2,1,0:T(8,128)(2,1)} %bitcast.14), channel_id=1, source_target_pairs={{0,4},{4,8},{8,12},{12,16},{16,20},{20,24},{24,28},{28,0},{1,5},{5... | collective-permute-start | bytes 3145736 | tf_op jit(solution)/shard_map/ppermute | solution.py:29
  52.7 1.1 %copy-start.1 = (f32[1,16,8192]{2,1,0:T(8,128)S(1)}, f32[1,16,8192]{2,1,0:T(8,128)}, u32[]{:S(2)}) copy-start(f32[1,16,8192]{2,1,0:T(8,128)} %param.8) | copy-start | bytes 1572868
  69.7 3.9 %copy-start.2 = (f32[16,64]{1,0:T(8,128)S(1)}, f32[16,64]{1,0:T(8,128)}, u32[]{:S(2)}) copy-start(f32[16,64]{1,0:T(8,128)} %param.13) | copy-start | bytes 12292
